TPU v7x, 32 devices: a whole 2x2x4 slice. The times are simulated.
32 devices in a mesh: groups: 2 (over x), tm: 16 (over z, y, core).
Axes of the slice: x: 2, y: 2, z: 4, core: 2. Of those that a mesh axis runs over, the one named last changes fastest.
Arguments:
- loglik: float32 [4, 1024, 512], P('groups', None, 'tm'), parts along dimension 0, may hold values from -105 to 105
- trans_weight: float32 [256, 256], replicated, may hold values from 0 to 1, as said below
- block_mask: int32 [4, 4], replicated, may hold values from 0 to 1, as said below
- init_weight: float32 [256], replicated, may hold values from 0.01 to 1
- lengths: int32 [4], P('groups'), parts along dimension 0, may hold values from 512 to 1024, as said below
- pdf_map: int32 [256], replicated, may hold values from 0 to 511
Outputs:
- log_forward: float32 [4, 1024, 256], P('groups', 'tm'), parts along dimension 0
- log_gain: float32 [4, 1024], P('groups', 'tm'), parts along dimension 0
There are 2 independent parts, one for each index of `groups`. A program takes and returns all parts, laid end to end along the dimension named above; an argument that names none is the same for every part. Nothing has to cross between parts.
Inputs may be any that keep to these rules, and one draw needn't show every extreme that they name: `block_mask`: the diagonal blocks are always allowed. `lengths`: some utterance has all 1024 frames. `trans_weight`: every entry is positive.
All inputs are finite; a program needn't handle non-finite values.
Results may differ from a plain program's by a relative error of at most 0.0003.
Values sent between devices are 32-bit elements; how exact they have to be, the bound alone decides.
No kernel may reach another device: no remote copies, remote signals or barrier semaphores. Data moves between devices by JAX's collectives and lax.ppermute only.
A program may use at most 128 MiB of HBM per device.

v0:
```python
import jax
import jax.numpy as jnp
from jax import lax
from jax.sharding import PartitionSpec as P


def carried_in(part, axis, combine, identity):
    place = lax.axis_index(axis)
    gathered = lax.all_gather(part, axis)
    state = jnp.zeros_like(part) + jnp.asarray(identity, part.dtype)

    def one(turn, state):
        return combine(state, lax.dynamic_index_in_dim(gathered, turn, 0, False))

    return lax.fori_loop(0, place, one, state)


def transitions(trans_weight, block_mask):
    width = trans_weight.shape[0] // block_mask.shape[0]
    expanded = jnp.repeat(jnp.repeat(block_mask, width, axis=0), width, axis=1).astype(jnp.float32)
    masked = trans_weight * expanded
    return masked / jnp.sum(masked, axis=1, keepdims=True)


def rescale(matrix):
    return matrix / jnp.max(matrix, axis=(1, 2), keepdims=True)


def chain_product(earlier, later):
    joined = jnp.einsum("uij,ujk->uik", earlier, later, precision=lax.Precision.HIGHEST)
    return rescale(joined)


def shards(loglik, trans_weight, block_mask, init_weight, lengths, pdf_map):
    trans = transitions(trans_weight, block_mask)
    states = trans.shape[0]
    utts = loglik.shape[0]
    start = init_weight / jnp.sum(init_weight)
    g_vals = jnp.take(
        lax.all_to_all(loglik, "tm", split_axis=1, concat_axis=2, tiled=True), pdf_map, axis=2
    )
    top = jnp.max(g_vals, axis=2, keepdims=True)
    factors = jnp.exp(g_vals - top)
    tops = top[..., 0]
    frame_count = factors.shape[1]
    offset = lax.axis_index("tm") * frame_count
    frame_ids = offset + jnp.arange(frame_count, dtype=jnp.int32)
    live = frame_ids[None, :] < lengths[:, None]
    seq_factors = jnp.moveaxis(factors, 1, 0)
    seq_tops = jnp.moveaxis(tops, 1, 0)
    seq_live = jnp.moveaxis(live, 1, 0)
    identity = jnp.broadcast_to(jnp.eye(states, dtype=jnp.float32), (utts, states, states))

    def extend(index, matrices):
        factor = lax.dynamic_index_in_dim(factors, index, 1, keepdims=False)
        alive = lax.dynamic_index_in_dim(live, index, 1, keepdims=False)
        step_op = jnp.where(alive[:, None, None], trans[None, :, :] * factor[:, None, :], identity)
        return chain_product(matrices, step_op)

    local_op = lax.fori_loop(0, frame_count, extend, identity)
    earlier_op = carried_in(local_op, "tm", chain_product, identity)
    incoming = jnp.einsum("i,uik->uk", start, earlier_op, precision=lax.Precision.HIGHEST)
    incoming = incoming / jnp.sum(incoming, axis=1, keepdims=True)

    def advance(alpha, inputs):
        factor, top, alive = inputs
        v_new = jnp.dot(alpha, trans, precision=lax.Precision.HIGHEST) * factor
        total = jnp.sum(v_new, axis=1, keepdims=True)
        fresh = jnp.where(alive[:, None], v_new / total, alpha)
        gain = jnp.where(alive, jnp.log(total[:, 0]) + top, jnp.float32(0.0))
        return (fresh, (fresh, gain))

    _, (occupied, gains) = lax.scan(advance, incoming, (seq_factors, seq_tops, seq_live))
    return (jnp.log(jnp.moveaxis(occupied, 0, 1)), jnp.moveaxis(gains, 0, 1))


def solution(mesh):
    return jax.shard_map(
        shards,
        mesh=mesh,
        in_specs=(P("groups", None, "tm"), P(), P(), P(), P("groups"), P()),
        out_specs=(P("groups", "tm", None), P("groups", "tm")),
        check_vma=False,
    )
```

profile of v0, /device:TPU:29, one launch (start us, length us, event | category | flops | bytes accessed | tf_op | source)
XLA Modules:
  0.0 243.3 jit_solution(11408980057508970936)
XLA Ops:
  7.2 1.4 copy.32
  8.6 1.7 reshape.49
  10.3 6.3 %all-to-all-start = ((f32[16,1,4096]{2,1,0:T(1,128)}), f32[16,1,4096]{2,1,0:T(1,128)S(1)}, u32[]{:S(2)}, u32[]{:S(2)}) async-start(f32[16,1,4096]{2,1,0:T(1,128)} %reshape.49), calls=%async_computation | async-start | bytes 524288 | tf_op jit(solution)/shard_map/all_to_all | solution.py:40
  21.0 2.7 %all-to-all-done = f32[16,1,4096]{2,1,0:T(1,128)S(1)} async-done(((f32[16,1,4096]{2,1,0:T(1,128)}), f32[16,1,4096]{2,1,0:T(1,128)S(1)}, u32[]{:S(2)}, u32[]{:S(2)}) %all-to-all-start) | async-done | bytes 262176 | tf_op jit(solution)/shard_map/all_to_all | solution.py:40
  24.2 1.3 reduce.2
  29.2 61.0 %while.40 = (s32[]{:T(128)}, f32[2,256,256]{1,2,0:T(8,128)S(1)}, pred[2,64]{0,1:T(8,128)(4,1)S(1)}, f32[256,256]{0,1:T(8,128)S(1)}, f32[2,64,256]{2,0,1:T(2,128)S(1)}, /*index=5*/f32[256,256]{0,1:T(8,128)S(1)}, s32[]{:T(128)}) while((s32[]{:T(128)}, f32[2,256,256]{1,2,0:T(8,128)S(1)}, pred[2,64]{0,1:T(8,128)(4,1)S(1)}, ...), condition=%wide.region_5.6_spmd.clone, body=%wide.region_3.5_spmd.clone.sunk | while | flops 403177472 | bytes 2627691 | solution.py:60
  93.4 71.4 %all-gather.3.cloned.1.call-done = f32[32,256,256]{2,1,0:T(8,128)} async-done(((f32[2,256,256]{2,1,0:T(8,128)}), f32[32,256,256]{2,1,0:T(8,128)}) %all-gather.3.cloned.1.call-update) | async-done | bytes 8388624 | tf_op jit(solution)/shard_map/all_gather | solution.py:9
  164.8 34.2 %while.38 = (s32[]{:T(128)}, f32[2,256,256]{1,2,0:T(8,128)S(1)}, s32[]{:T(128)}, f32[16,2,256,256]{3,2,1,0:T(8,128)}, s32[]{:T(128)}, /*index=5*/s32[]{:T(128)}, s32[]{:T(128)}) while((s32[]{:T(128)}, f32[2,256,256]{1,2,0:T(8,128)S(1)}, s32[]{:T(128)}, f32[16,2,256,256]{3,2,1,0:T(8,128)}, s32[]{:T(128)}, /*index=5*/s32[]{:T(128)}, ...), condition=%wide.region_8.9_spmd, body=%wide.region_6.8_spmd.sunk | while | flops 402915328 | bytes 2621571 | solution.py:15
  164.8 2.1 fusion.41
  167.1 2.1 fusion.41
  169.4 2.1 fusion.41
  171.7 2.1 fusion.41
  173.9 2.1 fusion.41
  176.2 2.1 fusion.41
  178.5 2.1 fusion.41
  180.8 2.1 fusion.41
  183.1 2.1 fusion.41
  185.3 2.1 fusion.41
  187.6 2.1 fusion.41
  189.9 2.1 fusion.41
  192.2 2.1 fusion.41
  194.5 2.1 fusion.41
  196.8 2.1 fusion.41
  199.7 35.4 %while.39 = (s32[]{:T(128)}, f32[2,256]{1,0:T(2,128)S(1)}, f32[64,2,256]{2,0,1:T(8,128)S(1)}, f32[64,2]{1,0:T(8,128)S(1)}, pred[64,2]{1,0:T(8,128)(4,1)S(1)}, /*...) while((s32[]{:T(128)}, f32[2,256]{1,0:T(2,128)S(1)}, ...), condition=%wide.region_12.13_spmd, body=%wide.region_10.12_spmd.sunk | while | flops 1574916 | bytes 282809 | solution.py:73
  (763 shorter events, 107.0 us)
Async XLA Ops:
  10.3 13.4 %all-to-all-start = ((f32[16,1,4096]{2,1,0:T(1,128)}), f32[16,1,4096]{2,1,0:T(1,128)S(1)}, u32[]{:S(2)}, u32[]{:S(2)}) async-start(f32[16,1,4096]{2,1,0:T(1,128)} %reshape.49), calls=%async_computation | async-start | bytes 524288 | tf_op jit(solution)/shard_map/all_to_all | solution.py:40
  16.7 148.1 %all-gather.3.cloned.1.call-start = ((), (), s32[]{:S(2)}) async-start(), calls=%async_computation.1 | async-start | bytes 8912896 | tf_op jit(solution)/shard_map/all_gather | solution.py:9
  29.0 62.5 %copy-start = (f32[256]{0:T(256)S(1)}, f32[256]{0:T(256)}, u32[]{:S(2)}) copy-start(f32[256]{0:T(256)} %param.15) | copy-start | bytes 3076
  29.0 63.7 %copy-start.1 = (s32[2]{0:T(128)S(1)}, s32[2]{0:T(128)}, u32[]{:S(2)}) copy-start(s32[2]{0:T(128)} %param.16) | copy-start | bytes 28
Sparse Core Ops, SparseCore 0:
  91.4 73.2 all-gather.2
where the time goes:
time: 244 us; the launch traced here: 243 us
  matrix products  104 us (43%)
  waiting for transfers between devices  74.1 us (30%)
  other arithmetic  21.8 us (9%)
  local copies, waits for them, and re-layouts  17.6 us (7%)
  between operations  14.2 us (6%)
  starting transfers between devices  6.37 us (3%)
  loops' own time  5.33 us (2%)
    dot_general x79, matrix products, chain_product(): jnp.einsum('uij,ujk->uik', earlier, later, precision=lax.Precision.HIGHEST)  82 us
    all_gather x1, waiting for transfers between devices, carried_in(): gathered = lax.all_gather(part, axis)  71.4 us
    dot_general x64, matrix products, advance(): v_new = jnp.dot(alpha, trans, precision=lax.Precision.HIGHEST) * factor  21.3 us
    div x79, other arithmetic, rescale(): return matrix / jnp.max(matrix, axis=(1, 2), keepdims=True)  8.92 us
    all_to_all x1, starting transfers between devices, shards(): lax.all_to_all(loglik, 'tm', split_axis=1, concat_axis=2, tiled=True)  6.33 us
    unnamed x9, local copies, waits for them, and re-layouts  5.28 us
    select_n x64, other arithmetic, advance(): fresh = jnp.where(alive[:, None], v_new / total, alpha)  5.19 us
  transfers between devices with their start and end apart: 2, of which 2 were waited for; matrix products, arithmetic and copies ran while one was open for 3% of the time, Pallas kernels for 0%

commit v1 on v0

--- a/solution.py
+++ b/solution.py
@@ -37,7 +37,12 @@
     utts = loglik.shape[0]
     start = init_weight / jnp.sum(init_weight)
     g_vals = jnp.take(
-        lax.all_to_all(loglik, "tm", split_axis=1, concat_axis=2, tiled=True), pdf_map, axis=2
+        jnp.concatenate(
+            lax.all_to_all(jnp.stack(jnp.split(loglik, lax.axis_size("tm"), axis=1)), "tm", 0, 0),
+            axis=2,
+        ),
+        pdf_map,
+        axis=2,
     )
     top = jnp.max(g_vals, axis=2, keepdims=True)
     factors = jnp.exp(g_vals - top)

time: 244 us -> 255 us (1.045)
  local copies, waits for them, and re-layouts: 17.6 us -> 27.2 us
    unnamed x9 -> x23, local copies, waits for them, and re-layouts: 5.28 us -> 14.4 us
  transfers between devices with their start and end apart: 2 -> 2, of which waited for: 2 -> 2; matrix products, arithmetic and copies ran while one was open for 3% -> 2% of each run, Pallas kernels for 0% -> 0%
where the time goes in v1:
time: 255 us; the launch traced here: 253 us
  matrix products  104 us (41%)
  waiting for transfers between devices  74.1 us (29%)
  local copies, waits for them, and re-layouts  27.2 us (11%)
  other arithmetic  21.8 us (9%)
  between operations  14.2 us (6%)
  starting transfers between devices  6.37 us (2%)
  loops' own time  5.33 us (2%)
    dot_general x79, matrix products, chain_product(): jnp.einsum('uij,ujk->uik', earlier, later, precision=lax.Precision.HIGHEST)  82 us
    all_gather x1, waiting for transfers between devices, carried_in(): gathered = lax.all_gather(part, axis)  71.4 us
    dot_general x64, matrix products, advance(): v_new = jnp.dot(alpha, trans, precision=lax.Precision.HIGHEST) * factor  21.3 us
    unnamed x23, local copies, waits for them, and re-layouts  14.4 us
    div x79, other arithmetic, rescale(): return matrix / jnp.max(matrix, axis=(1, 2), keepdims=True)  8.92 us
    all_to_all x1, starting transfers between devices, shards(): lax.all_to_all(jnp.stack(jnp.split(loglik, lax.axis_size('tm'), axis=1)),...  6.33 us
    select_n x64, other arithmetic, advance(): fresh = jnp.where(alive[:, None], v_new / total, alpha)  5.19 us
  transfers between devices with their start and end apart: 2, of which 2 were waited for; matrix products, arithmetic and copies ran while one was open for 2% of the time, Pallas kernels for 0%

profile of v1, /device:TPU:29, one launch (start us, length us, event | category | flops | bytes accessed | tf_op | source)
XLA Modules:
  0.0 252.9 jit_solution(10340044332833420688)
XLA Ops:
  21.0 6.3 %all-to-all-start = ((f32[16,1,4096]{2,1,0:T(1,128)}), f32[16,1,4096]{2,1,0:T(1,128)S(1)}, u32[]{:S(2)}, u32[]{:S(2)}) async-start(f32[16,1,4096]{2,1,0:T(1,128)} %reshape.57), calls=%async_computation | async-start | bytes 524288 | tf_op jit(solution)/shard_map/all_to_all | solution.py:41
  28.1 1.1 copy.31
  31.6 2.7 %all-to-all-done = f32[16,1,4096]{2,1,0:T(1,128)S(1)} async-done(((f32[16,1,4096]{2,1,0:T(1,128)}), f32[16,1,4096]{2,1,0:T(1,128)S(1)}, u32[]{:S(2)}, u32[]{:S(2)}) %all-to-all-start) | async-done | bytes 262176 | tf_op jit(solution)/shard_map/all_to_all | solution.py:41
  34.8 1.3 reduce.2
  38.7 61.0 %while.40 = (s32[]{:T(128)}, f32[2,256,256]{1,2,0:T(8,128)S(1)}, pred[2,64]{0,1:T(8,128)(4,1)S(1)}, f32[256,256]{0,1:T(8,128)S(1)}, f32[2,64,256]{2,0,1:T(2,128)S(1)}, /*index=5*/f32[256,256]{0,1:T(8,128)S(1)}, s32[]{:T(128)}) while((s32[]{:T(128)}, f32[2,256,256]{1,2,0:T(8,128)S(1)}, pred[2,64]{0,1:T(8,128)(4,1)S(1)}, ...), condition=%wide.region_5.6_spmd.clone, body=%wide.region_3.5_spmd.clone.sunk | while | flops 403177472 | bytes 2627691 | solution.py:65
  99.8 1.0 copy.35
  102.9 71.4 %all-gather.3.cloned.1.call-done = f32[32,256,256]{2,1,0:T(8,128)} async-done(((f32[2,256,256]{2,1,0:T(8,128)}), f32[32,256,256]{2,1,0:T(8,128)}) %all-gather.3.cloned.1.call-update) | async-done | bytes 8388624 | tf_op jit(solution)/shard_map/all_gather | solution.py:9
  174.3 34.2 %while.38 = (s32[]{:T(128)}, f32[2,256,256]{1,2,0:T(8,128)S(1)}, s32[]{:T(128)}, f32[16,2,256,256]{3,2,1,0:T(8,128)}, s32[]{:T(128)}, /*index=5*/s32[]{:T(128)}, s32[]{:T(128)}) while((s32[]{:T(128)}, f32[2,256,256]{1,2,0:T(8,128)S(1)}, s32[]{:T(128)}, f32[16,2,256,256]{3,2,1,0:T(8,128)}, s32[]{:T(128)}, /*index=5*/s32[]{:T(128)}, ...), condition=%wide.region_8.9_spmd, body=%wide.region_6.8_spmd.sunk | while | flops 402915328 | bytes 2621571 | solution.py:15
  174.4 2.1 fusion.41
  176.7 2.1 fusion.41
  178.9 2.1 fusion.41
  181.2 2.1 fusion.41
  183.5 2.1 fusion.41
  185.8 2.1 fusion.41
  188.1 2.1 fusion.41
  190.3 2.1 fusion.41
  192.6 2.1 fusion.41
  194.9 2.1 fusion.41
  197.2 2.1 fusion.41
  199.5 2.1 fusion.41
  201.7 2.1 fusion.41
  204.0 2.1 fusion.41
  206.3 2.1 fusion.41
  209.3 35.4 %while.39 = (s32[]{:T(128)}, f32[2,256]{1,0:T(2,128)S(1)}, f32[64,2,256]{2,0,1:T(8,128)S(1)}, f32[64,2]{1,0:T(8,128)S(1)}, pred[64,2]{1,0:T(8,128)(4,1)S(1)}, /*...) while((s32[]{:T(128)}, f32[2,256]{1,0:T(2,128)S(1)}, ...), condition=%wide.region_12.13_spmd, body=%wide.region_10.12_spmd.sunk | while | flops 1574916 | bytes 282809 | solution.py:78
  (779 shorter events, 117.5 us)
Async XLA Ops:
  21.0 13.4 %all-to-all-start = ((f32[16,1,4096]{2,1,0:T(1,128)}), f32[16,1,4096]{2,1,0:T(1,128)S(1)}, u32[]{:S(2)}, u32[]{:S(2)}) async-start(f32[16,1,4096]{2,1,0:T(1,128)} %reshape.57), calls=%async_computation | async-start | bytes 524288 | tf_op jit(solution)/shard_map/all_to_all | solution.py:41
  27.3 147.0 %all-gather.3.cloned.1.call-start = ((), (), s32[]{:S(2)}) async-start(), calls=%async_computation.1 | async-start | bytes 8912896 | tf_op jit(solution)/shard_map/all_gather | solution.py:9
  38.5 62.5 %copy-start = (f32[256]{0:T(256)S(1)}, f32[256]{0:T(256)}, u32[]{:S(2)}) copy-start(f32[256]{0:T(256)} %param.15) | copy-start | bytes 3076
  38.5 63.7 %copy-start.1 = (s32[2]{0:T(128)S(1)}, s32[2]{0:T(128)}, u32[]{:S(2)}) copy-start(s32[2]{0:T(128)} %param.16) | copy-start | bytes 28
Sparse Core Ops, SparseCore 0:
  101.0 73.2 all-gather.2
